TPU v7x, 256 devices: a whole 4x4x8 slice. The times are simulated.
256 devices in a mesh: seq: 64 (over z, y, core), grp: 4 (over x).
Axes of the slice: x: 4, y: 4, z: 8, core: 2. Of those that a mesh axis runs over, the one named last changes fastest.
Arguments:
- q_nope: bfloat16 [1024, 128, 128], P('seq', 'grp'), may hold values from -6 to 6
- q_rope: bfloat16 [1024, 128, 64], P('seq', 'grp'), may hold values from -256 to 256
- cache: bfloat16 [65536, 576], P('seq'), may hold values from -6 to 6
- w_uk: bfloat16 [128, 65536], P('grp', 'seq'), may hold values from -0.5 to 0.5
- w_uv: bfloat16 [128, 65536], P('grp', 'seq'), may hold values from -0.25 to 0.25
- d_out: bfloat16 [1024, 128, 128], P('seq', 'grp'), may hold values from -6 to 6
- sel: int32 [1024, 32], P('seq'), may hold values from 0 to 63, as said below
- slot_blocks: int32 [64, 64], P('seq'), may hold values from 0 to 15, as said below
Outputs:
- attn_out: bfloat16 [1024, 128, 128], P('seq', 'grp')
- d_q_nope: bfloat16 [1024, 128, 128], P('seq', 'grp')
- d_q_rope: bfloat16 [1024, 128, 64], P('seq', 'grp')
- d_cache: float32 [65536, 576], P('seq')
Inputs may be any that keep to these rules, and one draw needn't show every extreme that they name: `sel`: each row names 32 different places; place s stands for the block that the row's device asks of device s. `slot_blocks`: entry [r, s] is the index among device s's own blocks of the block that device r asks for in place s; the 1 entries of a row toward one device differ.
All inputs are finite; a program needn't handle non-finite values.
Results may differ from a plain program's by a relative error of at most 0.015.
Values may be sent and summed in bfloat16 or wider, within the bound.
A program may use at most 128 MiB of HBM per device.

v0:
```python
import math
import jax
import jax.numpy as jnp
from jax import lax
from jax.sharding import PartitionSpec as P

BLOCK_LEN = 64


def local(q_nope, q_rope, cache, w_uk, w_uv, d_out, sel, slot_blocks):
    peers = lax.axis_size("seq")
    queries, heads, nope = q_nope.shape
    rope = q_rope.shape[2]
    width = cache.shape[1]
    latent = width - rope
    value = d_out.shape[2]
    slot_total = slot_blocks.shape[1]
    per_peer = slot_total // peers
    own_blocks = cache.shape[0] // BLOCK_LEN
    scale = 1.0 / math.sqrt(nope + rope)
    gathered_k, gathered_v = (
        lax.all_gather(w_uk, "seq", axis=1, tiled=True),
        lax.all_gather(w_uv, "seq", axis=1, tiled=True),
    )
    weight_k = gathered_k.reshape(heads, nope, latent)
    weight_v = gathered_v.reshape(heads, latent, value)
    wanted = slot_blocks.reshape(peers, per_peer)
    asked = lax.all_to_all(wanted, "seq", split_axis=0, concat_axis=0, tiled=True)
    blocks = cache.reshape(own_blocks, BLOCK_LEN, width)
    arrived = lax.all_to_all(blocks[asked], "seq", split_axis=0, concat_axis=0, tiled=True)
    keys = arrived.reshape(slot_total * BLOCK_LEN, width)
    keys_lat = keys[:, :latent]
    q_lat = jnp.einsum("qhn,hnl->qhl", q_nope, weight_k, preferred_element_type=jnp.float32).astype(
        jnp.bfloat16
    )
    qfull = jnp.concatenate([q_lat, q_rope], axis=-1)
    chosen = jnp.any(
        sel[:, :, None] == jnp.arange(slot_total, dtype=jnp.int32)[None, None, :], axis=1
    )
    live = jnp.repeat(chosen, BLOCK_LEN, axis=1)[:, None, :]
    score = jnp.einsum("qhc,tc->qht", qfull, keys, preferred_element_type=jnp.float32) * scale
    score = jnp.where(live, score, -jnp.inf)
    prob = jax.nn.softmax(score, axis=-1)
    prob_low = prob.astype(jnp.bfloat16)
    olat = jnp.einsum("qht,tl->qhl", prob_low, keys_lat, preferred_element_type=jnp.float32).astype(
        jnp.bfloat16
    )
    attn_out = jnp.einsum(
        "qhl,hlv->qhv", olat, weight_v, preferred_element_type=jnp.float32
    ).astype(jnp.bfloat16)
    d_olat = jnp.einsum("qhv,hlv->qhl", d_out, weight_v, preferred_element_type=jnp.float32).astype(
        jnp.bfloat16
    )
    dprob = jnp.einsum("qhl,tl->qht", d_olat, keys_lat, preferred_element_type=jnp.float32)
    delta = jnp.sum(prob * dprob, axis=-1, keepdims=True)
    dscore = (prob * (dprob - delta) * scale).astype(jnp.bfloat16)
    dquery = jnp.einsum("qht,tc->qhc", dscore, keys, preferred_element_type=jnp.float32)
    d_q_rope = dquery[:, :, latent:].astype(jnp.bfloat16)
    d_qlat = dquery[:, :, :latent].astype(jnp.bfloat16)
    d_q_nope = jnp.einsum(
        "qhl,hnl->qhn", d_qlat, weight_k, preferred_element_type=jnp.float32
    ).astype(jnp.bfloat16)
    value_part = jnp.einsum("qht,qhl->tl", prob_low, d_olat, preferred_element_type=jnp.float32)
    dkeys = jnp.einsum("qht,qhc->tc", dscore, qfull, preferred_element_type=jnp.float32)
    dkeys = dkeys + jnp.pad(value_part, ((0, 0), (0, rope)))
    one_hot = (
        asked.reshape(-1)[:, None] == jnp.arange(own_blocks, dtype=jnp.int32)[None, :]
    ).astype(jnp.float32)
    returned = lax.all_to_all(
        dkeys.reshape(peers, per_peer, BLOCK_LEN * width).astype(jnp.bfloat16),
        "seq",
        split_axis=0,
        concat_axis=0,
        tiled=True,
    ).astype(jnp.float32)
    local_grad = jnp.dot(
        one_hot.T,
        returned.reshape(peers * per_peer, BLOCK_LEN * width),
        precision=lax.Precision.HIGHEST,
    )
    d_cache = (
        lax.psum(local_grad.astype(jnp.bfloat16), "grp")
        .astype(jnp.float32)
        .reshape(own_blocks * BLOCK_LEN, width)
    )
    return (attn_out, d_q_nope, d_q_rope, d_cache)


def solution(mesh):
    return jax.shard_map(
        local,
        mesh=mesh,
        in_specs=(
            P("seq", "grp", None),
            P("seq", "grp", None),
            P("seq", None),
            P("grp", "seq"),
            P("grp", "seq"),
            P("seq", "grp", None),
            P("seq", None),
            P("seq", None),
        ),
        out_specs=(
            P("seq", "grp", None),
            P("seq", "grp", None),
            P("seq", "grp", None),
            P("seq", None),
        ),
        check_vma=False,
    )
```

profile of v0, /device:TPU:8, one launch (start us, length us, event | category | flops | bytes accessed | tf_op | source)
XLA Modules:
  0.0 523.4 jit_solution(6179962597997448510)
XLA Ops:
  7.9 1.4 copy.80
  9.3 12.1 %all-to-all-start = ((s32[64,1,1]{2,1,0:T(1,128)}), s32[64,1,1]{2,1,0:T(1,128)S(1)}, u32[]{:S(2)}, u32[]{:S(2)}) async-start(s32[64,1,1]{2,1,0:T(1,128)} %copy.80), calls=%async_computation | async-start | bytes 65536 | tf_op jit(solution)/shard_map/all_to_all | solution.py:28
  21.4 1.7 copy.79
  23.1 6.9 %all-to-all-done = s32[64,1,1]{2,1,0:T(1,128)S(1)} async-done(((s32[64,1,1]{2,1,0:T(1,128)}), s32[64,1,1]{2,1,0:T(1,128)S(1)}, u32[]{:S(2)}, u32[]{:S(2)}) %all-to-all-start) | async-done | bytes 288 | tf_op jit(solution)/shard_map/all_to_all | solution.py:28
  29.9 2.4 fusion.49
  32.3 3.5 gather_fusion
  35.8 6.7 %all-to-all-start.1 = ((bf16[64,1,64,576]{3,2,1,0:T(8,128)(2,1)}), bf16[64,1,64,576]{3,2,1,0:T(8,128)(2,1)}, u32[]{:S(2)}, u32[]{:S(2)}) async-start(bf16[64,1,64,576]{3,2,1,0:T(8,128)(2,1)} %bitcast.47), calls=%async_computation.1 | async-start | bytes 10485760 | tf_op jit(solution)/shard_map/all_to_all | solution.py:30
  43.9 67.8 %all-gather.5.cloned.1.call-done = bf16[32,65536]{1,0:T(8,128)(2,1)} async-done(((bf16[32,1024]{1,0:T(8,128)(2,1)}), bf16[32,65536]{1,0:T(8,128)(2,1)}) %all-gather.5.cloned.1.call-update) | async-done | bytes 4194320 | tf_op jit(solution)/shard_map/all_gather | solution.py:23
  111.7 5.1 copy.102
  116.8 78.3 %all-gather.3.cloned.1.call-done = bf16[32,65536]{1,0:T(8,128)(2,1)} async-done(((bf16[32,1024]{1,0:T(8,128)(2,1)}), bf16[32,65536]{1,0:T(8,128)(2,1)}) %all-gather.3.cloned.1.call-update) | async-done | bytes 4194320 | tf_op jit(solution)/shard_map/all_gather | solution.py:22
  195.1 3.9 copy.101
  199.0 2.1 copy-done.3
  201.8 1.2 fusion.27
  203.0 8.0 %fusion.12 = f32[16,32,4096]{2,1,0:T(8,128)} fusion(bf16[4096,576]{1,0:T(8,128)(2,1)} %bitcast.5, bf16[16,32,512]{2,0,1:T(8,128)(2,1)S(1)} %fusion.27), kind=kOutput, calls=%fused_computation.20 | convolution fusion | flops 2147483648 | bytes 13107200 | tf_op jit(solution)/shard_map/qhl,tl->qht/dot_general | solution.py:54
  211.0 10.7 %fusion.50 = (f32[16,32]{1,0:T(8,128)S(1)}, f32[16,32,4096]{2,1,0:T(8,128)}) fusion(pred[16,4096]{1,0:T(8,128)(4,1)S(1)} %broadcast_in_dim.25, bf16[4096,576,1]{1,0,2:T(8,128)(2,1)} %bitcast.6, bf16[16,32,576]{2,0,1:T(8,128)(2,1)S(1)} %pad_maximum_fusion), kind=kOutput, calls=%fused_computation.59 | convolution fusion | flops 2424311808 | bytes 13764608 | tf_op jit(solution)/shard_map/sub | solution.py:43
  221.7 9.4 %convolution_bitcast_fusion = f32[4096,512]{0,1:T(8,128)} fusion(bf16[16,32,512]{2,0,1:T(8,128)(2,1)S(1)} %fusion.27, f32[16,32,4096]{2,1,0:T(8,128)} %get-tuple-element.27, f32[16,32]{1,0:T(8,128)S(1)} %get-tuple-element.26), kind=kOutput, calls=%fused_computation.12 | convolution fusion | flops 2151677952 | bytes 17303552 | tf_op jit(solution)/shard_map/qht,qhl->tl/dot_general | solution.py:63
  231.1 18.8 %fusion.2 = bf16[4096,576]{0,1:T(8,128)(2,1)} fusion(f32[4096,512]{0,1:T(8,128)} %convolution_bitcast_fusion, f32[16,32,4096]{2,1,0:T(8,128)} %fusion.12, bf16[16,32,576]{2,0,1:T(8,128)(2,1)S(1)} %pad_maximum_fusion, f32[16,32,4096]{2,1,0:T(8,128)} %get-tuple-element.27, f32[16,32]{1,0:T(8,128)S(1)} %get-tuple-element.26), kind=kOutput, calls=%fused_computation.5 | convolution fusion | flops 2435322368 | bytes 30476288 | tf_op jit(solution)/shard_map/qht,qhc->tc/dot_general | solution.py:64
  249.9 7.6 %copy.91 = bf16[4096,576]{1,0:T(8,128)(2,1)} copy(bf16[4096,576]{0,1:T(8,128)(2,1)} %fusion.2) | data formatting | bytes 9437184 | tf_op jit(solution)/shard_map/convert_element_type | solution.py:70
  257.5 21.7 %convert_element_type.71 = bf16[64,1,36864]{2,1,0:T(2,128)(2,1)} reshape(bf16[4096,576]{1,0:T(8,128)(2,1)} %copy.91) | data formatting | bytes 9437184 | tf_op jit(solution)/shard_map/convert_element_type | solution.py:70
  279.7 29.9 %reduce.4 = bf16[64,36864]{1,0:T(8,128)(2,1)} reduce(bf16[64,1,36864]{2,1,0:T(2,128)(2,1)} %convert_element_type.71, bf16[]{:T(256)} %broadcast.36), dimensions={1}, to_apply=%convert_element_type.71.reduce_sub_computation | reduce | bytes 9437186 | tf_op jit(solution)/shard_map/convert_element_type | solution.py:70
  309.7 8.3 %reshape.84 = bf16[64,2,18432]{2,1,0:T(2,128)(2,1)} reshape(bf16[64,36864]{1,0:T(8,128)(2,1)} %reduce.4) | data formatting | bytes 9437184
  317.9 8.0 %all-to-all-start.2 = ((bf16[64,2,18432]{2,1,0:T(2,128)(2,1)}), bf16[64,2,18432]{2,1,0:T(2,128)(2,1)}, u32[]{:S(2)}, u32[]{:S(2)}) async-start(bf16[64,2,18432]{2,1,0:T(2,128)(2,1)} %reshape.84), calls=%async_computation.2 | async-start | bytes 9437184 | tf_op jit(solution)/shard_map/all_to_all | solution.py:69
  326.2 7.0 %fusion.24 = bf16[16,32,512]{2,1,0:T(8,128)(2,1)S(1)} fusion(bf16[4096,576]{1,0:T(8,128)(2,1)} %bitcast.5, f32[16,32,4096]{2,1,0:T(8,128)} %get-tuple-element.27, f32[16,32]{1,0:T(8,128)S(1)} %get-tuple-element.26), kind=kOutput, calls=%fused_computation.26 | convolution fusion | flops 2151940096 | bytes 13109248 | tf_op jit(solution)/shard_map/qht,tl->qhl/dot_general | solution.py:45
  333.2 100.1 %all-to-all-done.2 = bf16[64,2,18432]{2,1,0:T(2,128)(2,1)} async-done(((bf16[64,2,18432]{2,1,0:T(2,128)(2,1)}), bf16[64,2,18432]{2,1,0:T(2,128)(2,1)}, u32[]{:S(2)}, u32[]{:S(2)}) %all-to-all-start.2) | async-done | bytes 4718624 | tf_op jit(solution)/shard_map/all_to_all | solution.py:69
  433.3 20.2 %reshape.85 = bf16[64,1,36864]{2,1,0:T(2,128)(2,1)} reshape(bf16[64,2,18432]{2,1,0:T(2,128)(2,1)} %all-to-all-done.2) | data formatting | bytes 9437184
  453.4 8.8 %convolution_convert_fusion = bf16[16,36864]{1,0:T(8,128)(2,1)S(1)} fusion(bf16[64,1,36864]{2,1,0:T(2,128)(2,1)} %reshape.85, s32[64]{0:T(128)S(1)} %get-tuple-element.24), kind=kOutput, calls=%fused_computation.3 | convolution fusion | flops 76088320 | bytes 5898496 | tf_op jit(solution)/shard_map/dot_general | solution.py:76
  462.2 2.5 reshape.67
  464.7 14.8 %fusion.21 = bf16[16,32,576]{2,1,0:T(8,128)(2,1)S(1)} fusion(bf16[4096,576,1]{1,0,2:T(8,128)(2,1)} %bitcast.6, f32[16,32,4096]{2,1,0:T(8,128)} %fusion.12, f32[16,32,4096]{2,1,0:T(8,128)} %get-tuple-element.27, f32[16,32]{1,0:T(8,128)S(1)} %get-tuple-element.26), kind=kOutput, calls=%fused_computation.25 | convolution fusion | flops 2430898688 | bytes 22087680 | tf_op jit(solution)/shard_map/qht,tc->qhc/dot_general | solution.py:57
  480.2 3.5 fusion.29
  484.4 1.2 fusion.30
  486.3 27.6 %all-reduce.3.cloned.1.call-done = bf16[1024,576]{1,0:T(8,128)(2,1)} async-done(((bf16[1024,576]{1,0:T(8,128)(2,1)}), bf16[1024,576]{1,0:T(8,128)(2,1)}) %all-reduce.3.cloned.1.call-update) | async-done | bytes 1179664 | tf_op jit(solution)/shard_map/psum | solution.py:82
  513.9 2.7 copy.95
  (34 shorter events, 5.8 us)
Async XLA Ops:
  7.2 194.6 %copy-start = (bf16[16,32,128]{2,1,0:T(8,128)(2,1)S(1)}, bf16[16,32,128]{2,1,0:T(8,128)(2,1)}, u32[]{:S(2)}) copy-start(bf16[16,32,128]{2,1,0:T(8,128)(2,1)} %param.13) | copy-start | bytes 393220
  7.2 104.5 %all-gather.5.cloned.1.call-start = ((), (), s32[]{:S(2)}) async-start(), calls=%async_computation.4 | async-start | bytes 4259840 | tf_op jit(solution)/shard_map/all_gather | solution.py:23
  9.3 20.7 %all-to-all-start = ((s32[64,1,1]{2,1,0:T(1,128)}), s32[64,1,1]{2,1,0:T(1,128)S(1)}, u32[]{:S(2)}, u32[]{:S(2)}) async-start(s32[64,1,1]{2,1,0:T(1,128)} %copy.80), calls=%async_computation | async-start | bytes 65536 | tf_op jit(solution)/shard_map/all_to_all | solution.py:28
  35.8 7.4 %copy-start.7 = (s32[16,32]{1,0:T(8,128)S(1)}, s32[16,32]{1,0:T(8,128)}, u32[]{:S(2)}) copy-start(s32[16,32]{1,0:T(8,128)} %param.14) | copy-start | bytes 6148
  35.8 8.0 %copy-start.6 = (bf16[16,32,64]{2,1,0:T(8,128)(2,1)S(1)}, bf16[16,32,64]{2,1,0:T(8,128)(2,1)}, u32[]{:S(2)}) copy-start(bf16[16,32,64]{2,1,0:T(8,128)(2,1)} %param.9) | copy-start | bytes 196612
  35.8 167.2 %all-to-all-start.1 = ((bf16[64,1,64,576]{3,2,1,0:T(8,128)(2,1)}), bf16[64,1,64,576]{3,2,1,0:T(8,128)(2,1)}, u32[]{:S(2)}, u32[]{:S(2)}) async-start(bf16[64,1,64,576]{3,2,1,0:T(8,128)(2,1)} %bitcast.47), calls=%async_computation.1 | async-start | bytes 10485760 | tf_op jit(solution)/shard_map/all_to_all | solution.py:30
  42.5 152.7 %all-gather.3.cloned.1.call-start = ((), (), s32[]{:S(2)}) async-start(), calls=%async_computation.3 | async-start | bytes 4259840 | tf_op jit(solution)/shard_map/all_gather | solution.py:22
  116.8 84.3 %copy-start.5 = (bf16[16,32,128]{2,1,0:T(8,128)(2,1)S(1)}, bf16[16,32,128]{2,1,0:T(8,128)(2,1)}, u32[]{:S(2)}) copy-start(bf16[16,32,128]{2,1,0:T(8,128)(2,1)} %param.8) | copy-start | bytes 393220
  195.1 6.7 %copy-start.2 = (bf16[4,8,512,128]{3,2,1,0:T(8,128)(2,1)S(1)}, bf16[4,8,512,128]{3,2,1,0:T(8,128)(2,1)}, u32[]{:S(2)}) copy-start(bf16[4,8,512,128]{3,2,1,0:T(8,128)(2,1)} %copy.102) | copy-start | bytes 12582916
  199.0 2.1 copy-start.3
  317.9 115.3 %all-to-all-start.2 = ((bf16[64,2,18432]{2,1,0:T(2,128)(2,1)}), bf16[64,2,18432]{2,1,0:T(2,128)(2,1)}, u32[]{:S(2)}, u32[]{:S(2)}) async-start(bf16[64,2,18432]{2,1,0:T(2,128)(2,1)} %reshape.84), calls=%async_computation.2 | async-start | bytes 9437184 | tf_op jit(solution)/shard_map/all_to_all | solution.py:69
  325.9 188.0 %all-reduce.3.cloned.1.call-start = ((), (), s32[]{:S(2)}) async-start(), calls=%async_computation.5 | async-start | bytes 2621440 | tf_op jit(solution)/shard_map/psum | solution.py:82
  479.5 5.0 copy-start.4
  480.2 36.4 %copy-start.1 = (bf16[16,32,128]{2,1,0:T(8,128)(2,1)S(1)}, bf16[16,32,128]{2,1,0:T(8,128)(2,1)}, u32[]{:S(2)}) copy-start(bf16[16,32,128]{2,1,0:T(8,128)(2,1)} %param.13) | copy-start | bytes 393220
Sparse Core Ops, SparseCore 0:
  10.8 100.8 all-gather.4
  114.5 80.5 all-gather.2
  464.8 49.0 all-reduce.2
where the time goes:
time: 529 us; the launch traced here: 523 us
  waiting for transfers between devices  282 us (53%)
  matrix products  84 us (16%)
  local copies, waits for them, and re-layouts  83.7 us (16%)
  other arithmetic  32.5 us (6%)
  starting transfers between devices  27.5 us (5%)
  between operations  14.1 us (3%)
    all_to_all x1, waiting for transfers between devices, local(): lax.all_to_all(dkeys.reshape(peers, per_peer, BLOCK_LEN * width).astype(j...  100 us
    all_gather x1, waiting for transfers between devices, local(): lax.all_gather(w_uk, 'seq', axis=1, tiled=True)  78.3 us
    all_gather x1, waiting for transfers between devices, local(): lax.all_gather(w_uv, 'seq', axis=1, tiled=True)  67.8 us
    unnamed x25, local copies, waits for them, and re-layouts  45.4 us
    convert_element_type x1, other arithmetic, local(): dkeys.reshape(peers, per_peer, BLOCK_LEN * width).astype(jnp.bfloat16)  29.9 us
    convert_element_type x3, local copies, waits for them, and re-layouts, local(): dkeys.reshape(peers, per_peer, BLOCK_LEN * width).astype(jnp.bfloat16)  29.9 us
    psum x1, waiting for transfers between devices, local(): lax.psum(local_grad.astype(jnp.bfloat16), 'grp').astype(jnp.float32)  27.6 us
    dot_general x1, matrix products, local(): jnp.einsum('qht,qhc->tc', dscore, qfull, preferred_element_type=jnp.float32)  18.8 us
  transfers between devices with their start and end apart: 6, of which 5 were waited for; matrix products, arithmetic and copies ran while one was open for 9% of the time, Pallas kernels for 0%

commit v1 on v0

--- a/solution.py
+++ b/solution.py
@@ -19,7 +19,9 @@
     own_blocks = cache.shape[0] // BLOCK_LEN
     scale = 1.0 / math.sqrt(nope + rope)
     gathered_k, gathered_v = (
-        lax.all_gather(w_uk, "seq", axis=1, tiled=True),
+        jnp.concatenate(
+            lax.all_to_all(jnp.stack([w_uk] * lax.axis_size("seq")), "seq", 0, 0), axis=1
+        ),
         lax.all_gather(w_uv, "seq", axis=1, tiled=True),
     )
     weight_k = gathered_k.reshape(heads, nope, latent)

time: 529 us -> 599 us (1.13)
  waiting for transfers between devices: 282 us -> 324 us
  blocking collectives: 0 us -> 20.5 us
  local copies, waits for them, and re-layouts: 83.7 us -> 94.2 us
  starting transfers between devices: 27.5 us -> 18.5 us
    all_to_all x1, waiting for transfers between devices: 6.86 us -> 89.6 us  [local(): lax.all_to_all(jnp.stack([w_uk] * lax.axis_size('seq')), 'seq', 0, 0)]
    all_gather x1 -> x0, waiting for transfers between devices: 78.3 us -> none  [local(): lax.all_gather(w_uk, 'seq', axis=1, tiled=True)]
    all_gather x1, waiting for transfers between devices: 67.8 us -> 98.3 us  [local(): lax.all_gather(w_uv, 'seq', axis=1, tiled=True)]
    all_to_all x0 -> x1, blocking collectives: none -> 20.5 us  [local(): lax.all_to_all(wanted, 'seq', split_axis=0, concat_axis=0, tiled=True)]
    another operation x0 -> x2, local copies, waits for them, and re-layouts: none -> 10.9 us  [the longest x1 7.64 us: local(): weight_k = gathered_k.reshape(heads, nope, latent)]
    all_to_all x1, waiting for transfers between devices: 0.01 us -> 7.32 us  [local(): lax.all_to_all(blocks[asked], 'seq', split_axis=0, concat_axis=0, tiled=T...]
    reshape x0 -> x1, local copies, waits for them, and re-layouts: none -> 6.54 us  [local(): jnp.concatenate(lax.all_to_all(jnp.stack([w_uk] * lax.axis_size('seq')),...]
    unnamed x25 -> x24, local copies, waits for them, and re-layouts: 45.4 us -> 39 us
  transfers between devices with their start and end apart: 6 -> 5, of which waited for: 5 -> 5; matrix products, arithmetic and copies ran while one was open for 9% -> 10% of each run, Pallas kernels for 0% -> 0%
where the time goes in v1:
time: 599 us; the launch traced here: 590 us
  waiting for transfers between devices  324 us (54%)
  local copies, waits for them, and re-layouts  94.2 us (16%)
  matrix products  86.3 us (14%)
  other arithmetic  32.5 us (5%)
  blocking collectives  20.5 us (3%)
  starting transfers between devices  18.5 us (3%)
  between operations  14.4 us (2%)
    all_to_all x1, waiting for transfers between devices, local(): lax.all_to_all(dkeys.reshape(peers, per_peer, BLOCK_LEN * width).astype(j...  100 us
    all_gather x1, waiting for transfers between devices, local(): lax.all_gather(w_uv, 'seq', axis=1, tiled=True)  98.3 us
    all_to_all x1, waiting for transfers between devices, local(): lax.all_to_all(jnp.stack([w_uk] * lax.axis_size('seq')), 'seq', 0, 0)  89.6 us
    unnamed x24, local copies, waits for them, and re-layouts  39 us
    convert_element_type x1, other arithmetic, local(): dkeys.reshape(peers, per_peer, BLOCK_LEN * width).astype(jnp.bfloat16)  29.9 us
    convert_element_type x3, local copies, waits for them, and re-layouts, local(): dkeys.reshape(peers, per_peer, BLOCK_LEN * width).astype(jnp.bfloat16)  29.9 us
    psum x1, waiting for transfers between devices, local(): lax.psum(local_grad.astype(jnp.bfloat16), 'grp').astype(jnp.float32)  27.5 us
    all_to_all x1, blocking collectives, local(): lax.all_to_all(wanted, 'seq', split_axis=0, concat_axis=0, tiled=True)  20.5 us
  transfers between devices with their start and end apart: 5, of which 5 were waited for; matrix products, arithmetic and copies ran while one was open for 10% of the time, Pallas kernels for 0%

profile of v1, /device:TPU:8, one launch (start us, length us, event | category | flops | bytes accessed | tf_op | source)
XLA Modules:
  0.0 590.2 jit_solution(8614910462081501529)
XLA Ops:
  8.0 20.5 %all_to_all.24 = s32[64,1,1]{2,1,0:T(1,128)S(1)} all-to-all(s32[64,1,1]{2,1,0:T(1,128)S(1)} %copy.83), channel_id=1, replica_groups=mesh['seq'=64,'grp'=4] {'seq'}, dimensions={0} | all-to-all | bytes 512 | tf_op jit(solution)/shard_map/all_to_all | solution.py:30
  28.5 3.3 stack.2
  31.8 6.6 %all-to-all-start = ((bf16[64,32,1024]{2,1,0:T(8,128)(2,1)}), bf16[64,32,1024]{2,1,0:T(8,128)(2,1)}, u32[]{:S(2)}, u32[]{:S(2)}) async-start(bf16[64,32,1024]{2,1,0:T(8,128)(2,1)} %stack.2), calls=%async_computation | async-start | bytes 8388608 | tf_op jit(solution)/shard_map/all_to_all | solution.py:23
  39.1 2.4 fusion.49
  41.5 3.5 gather_fusion
  45.0 89.6 %all-to-all-done = bf16[64,32,1024]{2,1,0:T(8,128)(2,1)} async-done(((bf16[64,32,1024]{2,1,0:T(8,128)(2,1)}), bf16[64,32,1024]{2,1,0:T(8,128)(2,1)}, u32[]{:S(2)}, u32[]{:S(2)}) %all-to-all-start) | async-done | bytes 4194336 | tf_op jit(solution)/shard_map/all_to_all | solution.py:23
  134.6 5.9 all-to-all-start.2
  141.9 98.3 %all-gather.2.cloned.1.call-done = bf16[32,65536]{1,0:T(8,128)(2,1)} async-done(((bf16[32,1024]{1,0:T(8,128)(2,1)}), bf16[32,65536]{1,0:T(8,128)(2,1)}) %all-gather.2.cloned.1.call-update) | async-done | bytes 4194320 | tf_op jit(solution)/shard_map/all_gather | solution.py:25
  240.2 5.1 copy.104
  245.3 6.5 %copy.79 = bf16[32,64,1024]{2,1,0:T(8,128)(2,1)} copy(bf16[32,64,1024]{2,0,1:T(8,128)(2,1)} %bitcast) | data formatting | bytes 8388608 | tf_op jit(solution)/shard_map/reshape | solution.py:22
  251.9 7.6 %reshape_reshape.3 = bf16[32,128,512]{2,1,0:T(8,128)(2,1)} reshape(bf16[32,64,1024]{2,1,0:T(8,128)(2,1)} %copy.79) | data formatting | bytes 8388608 | tf_op jit(solution)/shard_map/reshape;reshape | solution.py:27
  259.5 3.0 fusion.28
  264.1 7.3 %all-to-all-done.2 = bf16[64,1,64,576]{3,2,1,0:T(8,128)(2,1)} async-done(((bf16[64,1,64,576]{3,2,1,0:T(8,128)(2,1)}), bf16[64,1,64,576]{3,2,1,0:T(8,128)(2,1)}, u32[]{:S(2)}, u32[]{:S(2)}) %all-to-all-start.2) | async-done | bytes 4718624 | tf_op jit(solution)/shard_map/all_to_all | solution.py:32
  271.5 7.9 %fusion.12 = f32[16,32,4096]{2,1,0:T(8,128)} fusion(bf16[4096,576]{1,0:T(8,128)(2,1)} %bitcast.6, bf16[16,32,512]{2,0,1:T(8,128)(2,1)S(1)} %fusion.27), kind=kOutput, calls=%fused_computation.20 | convolution fusion | flops 2147483648 | bytes 13107200 | tf_op jit(solution)/shard_map/qhl,tl->qht/dot_general | solution.py:56
  279.4 10.7 %fusion.50 = (f32[16,32]{1,0:T(8,128)S(1)}, f32[16,32,4096]{2,1,0:T(8,128)}) fusion(pred[16,4096]{1,0:T(8,128)(4,1)S(1)} %broadcast_in_dim.25, bf16[4096,576,1]{1,0,2:T(8,128)(2,1)} %bitcast.7, bf16[16,32,576]{2,0,1:T(8,128)(2,1)S(1)} %pad_maximum_fusion), kind=kOutput, calls=%fused_computation.59 | convolution fusion | flops 2424311808 | bytes 13764608 | tf_op jit(solution)/shard_map/sub | solution.py:45
  290.1 9.2 %convolution_bitcast_fusion = f32[4096,512]{0,1:T(8,128)} fusion(bf16[16,32,512]{2,0,1:T(8,128)(2,1)S(1)} %fusion.27, f32[16,32,4096]{2,1,0:T(8,128)} %get-tuple-element.27, f32[16,32]{1,0:T(8,128)S(1)} %get-tuple-element.26), kind=kOutput, calls=%fused_computation.12 | convolution fusion | flops 2151677952 | bytes 17303552 | tf_op jit(solution)/shard_map/qht,qhl->tl/dot_general | solution.py:65
  299.3 19.0 %fusion.2 = bf16[4096,576]{0,1:T(8,128)(2,1)} fusion(f32[4096,512]{0,1:T(8,128)} %convolution_bitcast_fusion, f32[16,32,4096]{2,1,0:T(8,128)} %fusion.12, bf16[16,32,576]{2,0,1:T(8,128)(2,1)S(1)} %pad_maximum_fusion, f32[16,32,4096]{2,1,0:T(8,128)} %get-tuple-element.27, f32[16,32]{1,0:T(8,128)S(1)} %get-tuple-element.26), kind=kOutput, calls=%fused_computation.5 | convolution fusion | flops 2435322368 | bytes 30476288 | tf_op jit(solution)/shard_map/qht,qhc->tc/dot_general | solution.py:66
  318.3 7.6 %copy.94 = bf16[4096,576]{1,0:T(8,128)(2,1)} copy(bf16[4096,576]{0,1:T(8,128)(2,1)} %fusion.2) | data formatting | bytes 9437184 | tf_op jit(solution)/shard_map/convert_element_type | solution.py:72
  325.9 21.7 %convert_element_type.71 = bf16[64,1,36864]{2,1,0:T(2,128)(2,1)} reshape(bf16[4096,576]{1,0:T(8,128)(2,1)} %copy.94) | data formatting | bytes 9437184 | tf_op jit(solution)/shard_map/convert_element_type | solution.py:72
  348.2 29.9 %reduce.4 = bf16[64,36864]{1,0:T(8,128)(2,1)} reduce(bf16[64,1,36864]{2,1,0:T(2,128)(2,1)} %convert_element_type.71, bf16[]{:T(256)} %broadcast.38), dimensions={1}, to_apply=%convert_element_type.71.reduce_sub_computation | reduce | bytes 9437186 | tf_op jit(solution)/shard_map/convert_element_type | solution.py:72
  378.1 8.3 %reshape.86 = bf16[64,2,18432]{2,1,0:T(2,128)(2,1)} reshape(bf16[64,36864]{1,0:T(8,128)(2,1)} %reduce.4) | data formatting | bytes 9437184
  386.4 5.9 all-to-all-start.3
  392.3 7.0 %fusion.24 = bf16[16,32,512]{2,1,0:T(8,128)(2,1)S(1)} fusion(bf16[4096,576]{1,0:T(8,128)(2,1)} %bitcast.6, f32[16,32,4096]{2,1,0:T(8,128)} %get-tuple-element.27, f32[16,32]{1,0:T(8,128)S(1)} %get-tuple-element.26), kind=kOutput, calls=%fused_computation.26 | convolution fusion | flops 2151940096 | bytes 13109248 | tf_op jit(solution)/shard_map/qht,tl->qhl/dot_general | solution.py:47
  399.3 100.3 %all-to-all-done.3 = bf16[64,2,18432]{2,1,0:T(2,128)(2,1)} async-done(((bf16[64,2,18432]{2,1,0:T(2,128)(2,1)}), bf16[64,2,18432]{2,1,0:T(2,128)(2,1)}, u32[]{:S(2)}, u32[]{:S(2)}) %all-to-all-start.3) | async-done | bytes 4718624 | tf_op jit(solution)/shard_map/all_to_all | solution.py:71
  499.6 20.4 %reshape.87 = bf16[64,1,36864]{2,1,0:T(2,128)(2,1)} reshape(bf16[64,2,18432]{2,1,0:T(2,128)(2,1)} %all-to-all-done.3) | data formatting | bytes 9437184
  520.0 8.8 %convolution_convert_fusion = bf16[16,36864]{1,0:T(8,128)(2,1)S(1)} fusion(bf16[64,1,36864]{2,1,0:T(2,128)(2,1)} %reshape.87, s32[64]{0:T(128)S(1)} %get-tuple-element.24), kind=kOutput, calls=%fused_computation.3 | convolution fusion | flops 76088320 | bytes 5898496 | tf_op jit(solution)/shard_map/dot_general | solution.py:78
  528.7 2.5 reshape.69
  531.2 14.8 %fusion.21 = bf16[16,32,576]{2,1,0:T(8,128)(2,1)S(1)} fusion(bf16[4096,576,1]{1,0,2:T(8,128)(2,1)} %bitcast.7, f32[16,32,4096]{2,1,0:T(8,128)} %fusion.12, f32[16,32,4096]{2,1,0:T(8,128)} %get-tuple-element.27, f32[16,32]{1,0:T(8,128)S(1)} %get-tuple-element.26), kind=kOutput, calls=%fused_computation.25 | convolution fusion | flops 2430898688 | bytes 22087680 | tf_op jit(solution)/shard_map/qht,tc->qhc/dot_general | solution.py:59
  546.7 3.5 fusion.29
  551.0 1.2 fusion.30
  552.9 27.5 %all-reduce.3.cloned.1.call-done = bf16[1024,576]{1,0:T(8,128)(2,1)} async-done(((bf16[1024,576]{1,0:T(8,128)(2,1)}), bf16[1024,576]{1,0:T(8,128)(2,1)}) %all-reduce.3.cloned.1.call-update) | async-done | bytes 1179664 | tf_op jit(solution)/shard_map/psum | solution.py:84
  580.4 2.7 copy.98
  (34 shorter events, 7.3 us)
Async XLA Ops:
  7.2 255.4 %copy-start = (bf16[16,32,128]{2,1,0:T(8,128)(2,1)S(1)}, bf16[16,32,128]{2,1,0:T(8,128)(2,1)}, u32[]{:S(2)}) copy-start(bf16[16,32,128]{2,1,0:T(8,128)(2,1)} %param.13) | copy-start | bytes 393220
  31.8 6.6 %copy-start.4 = (bf16[1024,576]{0,1:T(8,128)(2,1)S(1)}, bf16[1024,576]{0,1:T(8,128)(2,1)}, u32[]{:S(2)}) copy-start(bf16[1024,576]{0,1:T(8,128)(2,1)} %param.10) | copy-start | bytes 3538948
  31.8 102.8 %all-to-all-start = ((bf16[64,32,1024]{2,1,0:T(8,128)(2,1)}), bf16[64,32,1024]{2,1,0:T(8,128)(2,1)}, u32[]{:S(2)}, u32[]{:S(2)}) async-start(bf16[64,32,1024]{2,1,0:T(8,128)(2,1)} %stack.2), calls=%async_computation | async-start | bytes 8388608 | tf_op jit(solution)/shard_map/all_to_all | solution.py:23
  134.6 6.6 %copy-start.7 = (s32[16,32]{1,0:T(8,128)S(1)}, s32[16,32]{1,0:T(8,128)}, u32[]{:S(2)}) copy-start(s32[16,32]{1,0:T(8,128)} %param.14) | copy-start | bytes 6148
  134.6 7.3 %copy-start.6 = (bf16[16,32,64]{2,1,0:T(8,128)(2,1)S(1)}, bf16[16,32,64]{2,1,0:T(8,128)(2,1)}, u32[]{:S(2)}) copy-start(bf16[16,32,64]{2,1,0:T(8,128)(2,1)} %param.9) | copy-start | bytes 196612
  134.6 136.9 %all-to-all-start.2 = ((bf16[64,1,64,576]{3,2,1,0:T(8,128)(2,1)}), bf16[64,1,64,576]{3,2,1,0:T(8,128)(2,1)}, u32[]{:S(2)}, u32[]{:S(2)}) async-start(bf16[64,1,64,576]{3,2,1,0:T(8,128)(2,1)} %bitcast.44), calls=%async_computation.2 | async-start | bytes 10485760 | tf_op jit(solution)/shard_map/all_to_all | solution.py:32
  140.5 99.7 %all-gather.2.cloned.1.call-start = ((), (), s32[]{:S(2)}) async-start(), calls=%async_computation.4 | async-start | bytes 4259840 | tf_op jit(solution)/shard_map/all_gather | solution.py:25
  251.9 7.7 %copy-start.5 = (bf16[16,32,128]{2,1,0:T(8,128)(2,1)S(1)}, bf16[16,32,128]{2,1,0:T(8,128)(2,1)}, u32[]{:S(2)}) copy-start(bf16[16,32,128]{2,1,0:T(8,128)(2,1)} %param.8) | copy-start | bytes 393220
  259.5 3.5 copy-start.3
  386.4 113.2 %all-to-all-start.3 = ((bf16[64,2,18432]{2,1,0:T(2,128)(2,1)}), bf16[64,2,18432]{2,1,0:T(2,128)(2,1)}, u32[]{:S(2)}, u32[]{:S(2)}) async-start(bf16[64,2,18432]{2,1,0:T(2,128)(2,1)} %reshape.86), calls=%async_computation.3 | async-start | bytes 9437184 | tf_op jit(solution)/shard_map/all_to_all | solution.py:71
  392.3 188.2 %all-reduce.3.cloned.1.call-start = ((), (), s32[]{:S(2)}) async-start(), calls=%async_computation.5 | async-start | bytes 2621440 | tf_op jit(solution)/shard_map/psum | solution.py:84
  546.0 5.0 copy-start.2
  546.7 36.4 %copy-start.1 = (bf16[16,32,128]{2,1,0:T(8,128)(2,1)S(1)}, bf16[16,32,128]{2,1,0:T(8,128)(2,1)}, u32[]{:S(2)}) copy-start(bf16[16,32,128]{2,1,0:T(8,128)(2,1)} %param.13) | copy-start | bytes 393220
Sparse Core Ops, SparseCore 0:
  144.1 96.0 all-gather.1
  531.3 49.0 all-reduce.2
